TPU v7x, 256 devices: a whole 4x4x8 slice. The times are simulated.
256 devices in a mesh: row: 16 (over x_hi, z), col: 16 (over y, x_lo, core).
Axes of the slice: x: 4 (x_hi: 2, x_lo: 2; x = x_hi * 2 + x_lo), y: 4, z: 8, core: 2. Of those that a mesh axis runs over, the one named last changes fastest.
Arguments:
- objective: float32 [256, 32768], P('row', 'col'), may hold values from -6 to 6
- center: bfloat16 [256, 32768], P('row', 'col'), may hold values from -5 to 5
- radius: bfloat16 [256, 32768], P('row', 'col'), may hold values from 0.049804688 to 1
- lower_gap: bfloat16 [3, 256, 32768], P(None, 'row', 'col'), may hold values from 0.19921875 to 3
- upper_gap: bfloat16 [3, 256, 32768], P(None, 'row', 'col'), may hold values from 0.19921875 to 3
- kernels: float32 [4, 3, 3, 64, 64], replicated, may hold values from -0.25 to 0.25
- biases: float32 [4, 64], replicated, may hold values from -3 to 3
- step_sizes: float32 [3], replicated, may hold values from 0.2 to 1
Outputs:
- bounds: float32 [3], replicated
- final_duals: float32 [3, 256, 32768], P(None, 'row', 'col')
- final_multipliers: float32 [3, 256, 32768], P(None, 'row', 'col')
All inputs are finite; a program needn't handle non-finite values.
Results may differ from a plain program's by a relative error of at most 0.0003.
Values sent between devices are 32-bit elements; how exact they have to be, the bound alone decides.
A program may use at most 128 MiB of HBM per device.

v0:
```python
import jax
import jax.numpy as jnp
from jax import lax
from jax.sharding import PartitionSpec as P

CH = 64
LAYERS = 4
ITERS = 3
TEMP = 0.5
EPS = 1e-06


def extended(cells, sides, width):
    for axis, dim in sides:
        count = lax.axis_size(axis)
        ends = count - 1
        head = lax.slice_in_dim(cells, 0, width, axis=dim)
        tail = lax.slice_in_dim(cells, cells.shape[dim] - width, cells.shape[dim], axis=dim)
        cells = jnp.concatenate(
            [
                lax.ppermute(tail, axis, [(i, (i + 1) % count) for i in range(ends)]),
                cells,
                lax.ppermute(head, axis, [((i + 1) % count, i) for i in range(ends)]),
            ],
            axis=dim,
        )
    return cells


def soft_value(coef, low, high):
    return coef * low - TEMP * jax.nn.softplus(coef * (low - high) / TEMP)


def soft_point(coef, low, high):
    return low + (high - low) * jax.nn.sigmoid(coef * (low - high) / TEMP)


def flipped(kernel):
    return jnp.transpose(kernel[::-1, ::-1], (0, 1, 3, 2))


def conv_valid(padded, kernel):
    out_rows = padded.shape[0] - 2
    out_cols = padded.shape[1] - 2
    in_chan = padded.shape[2]
    result = jnp.zeros((out_rows * out_cols, kernel.shape[3]), jnp.float32)
    for offset_row in range(3):
        for offset_col in range(3):
            window = padded[
                offset_row : offset_row + out_rows, offset_col : offset_col + out_cols
            ].reshape(out_rows * out_cols, in_chan)
            result = result + jnp.dot(
                window,
                kernel[offset_row, offset_col],
                precision=lax.Precision.HIGHEST,
                preferred_element_type=jnp.float32,
            )
    return result.reshape(out_rows, out_cols, kernel.shape[3])


def shards(objective, center, radius, lower_gap, upper_gap, kernels, biases, step_sizes):
    depth = LAYERS - 1
    tile_rows = objective.shape[0]
    tile_cols = objective.shape[1] // CH

    def cube(plane):
        return plane.reshape(plane.shape[:-1] + (tile_cols, CH))

    target = cube(objective)
    target_rim = extended(target, (("row", 0), ("col", 1)), 1)
    target_back = conv_valid(target_rim, flipped(kernels[LAYERS - 1]))
    fixed_part = jnp.sum(target * biases[LAYERS - 1])
    middle = cube(center.astype(jnp.float32))
    half = cube(radius.astype(jnp.float32))
    below = cube(lower_gap.astype(jnp.float32))
    above = cube(upper_gap.astype(jnp.float32))
    zero_map = jnp.zeros_like(middle)
    lows = [middle - half] + [zero_map] * depth
    highs = [middle + half] + [above[j] for j in range(depth)]
    duals = jnp.zeros((depth, tile_rows, tile_cols, CH), jnp.float32)
    multipliers = jnp.zeros_like(duals)
    total_cells = tile_rows * tile_cols * CH * lax.axis_size("row") * lax.axis_size("col")
    bounds = []
    for step in range(ITERS):
        coefs = []
        dual_rim = extended(duals, (("row", 1), ("col", 2)), 1)
        for layer in range(depth):
            coef = -conv_valid(dual_rim[layer], flipped(kernels[layer]))
            if layer > 0:
                coef = coef + multipliers[layer - 1]
            coefs.append(coef)
        points = [soft_point(coefs[layer], lows[layer], highs[layer]) for layer in range(depth)]
        primal = extended(jnp.stack(points), (("row", 1), ("col", 2)), 1)
        input_rims = [primal[layer] for layer in range(depth)]
        coefs.append(target_back + multipliers[depth - 1])
        points.append(soft_point(coefs[depth], lows[depth], highs[depth]))
        value = fixed_part
        for layer in range(LAYERS):
            value = value + jnp.sum(soft_value(coefs[layer], lows[layer], highs[layer]))
        slope_duals = []
        slope_mults = []
        squares = jnp.zeros((), jnp.float32)
        for j in range(depth):
            pos_coef = duals[j] - multipliers[j]
            neg_coef = -duals[j]
            value = value + jnp.sum(soft_value(pos_coef, zero_map, above[j]))
            value = value + jnp.sum(soft_value(neg_coef, zero_map, below[j]))
            value = value - jnp.sum(duals[j] * biases[j])
            positive = soft_point(pos_coef, zero_map, above[j])
            negative = soft_point(neg_coef, zero_map, below[j])
            slope_dual = positive - negative - conv_valid(input_rims[j], kernels[j]) - biases[j]
            slope_mult = points[j + 1] - positive
            squares = squares + jnp.sum(slope_dual * slope_dual) + jnp.sum(slope_mult * slope_mult)
            slope_duals.append(slope_dual)
            slope_mults.append(slope_mult)
        total_squares, total_value = lax.psum((squares, value), ("row", "col"))
        bounds.append(total_value / total_cells)
        scale = step_sizes[step] / jnp.sqrt(total_squares / (2 * depth * total_cells) + EPS)
        duals = duals + scale * jnp.stack(slope_duals)
        multipliers = multipliers + scale * jnp.stack(slope_mults)
    bound_array = jnp.stack(bounds)
    final_duals = duals.reshape(depth, tile_rows, tile_cols * CH)
    final_multipliers = multipliers.reshape(depth, tile_rows, tile_cols * CH)
    return (bound_array, final_duals, final_multipliers)


def solution(mesh):
    placed = (
        P("row", "col"),
        P("row", "col"),
        P("row", "col"),
        P(None, "row", "col"),
        P(None, "row", "col"),
        P(),
        P(),
        P(),
    )
    return jax.shard_map(
        shards,
        mesh=mesh,
        in_specs=placed,
        out_specs=(P(), P(None, "row", "col"), P(None, "row", "col")),
        check_vma=False,
    )
```

profile of v0, /device:TPU:1, one launch (start us, length us, event | category | flops | bytes accessed | tf_op | source)
XLA Modules:
  0.0 666.6 jit_solution(15798143236063260089)
XLA Ops:
  1.3 5.0 collective-permute-start
  8.5 4.0 collective-permute-start.4
  40.0 4.5 collective-permute-start.6
  54.1 2.1 collective-permute-start.2
  56.2 2.7 collective-permute-start.3
  86.0 4.3 collective-permute-start.8
  96.6 3.1 collective-permute-start.10
  101.9 2.3 multiply_reduce_fusion.14
  126.6 2.6 subtract_subtract_fusion.11
  133.0 88.6 %psum.43 = f32[]{:T(128)} all-reduce(f32[]{:T(128)S(6)} %add.1337), channel_id=1, replica_groups=mesh['row'=16,'col'=16] {'row','col'}, use_global_device_ids=true, to_apply=%region_21.22 | all-reduce | flops 1 | bytes 8 | tf_op jit(solution)/shard_map/psum | solution.py:116
  231.9 3.5 collective-permute-start.14
  235.4 2.3 collective-permute-start.15
  237.9 2.7 collective-permute-done.15
  260.7 2.4 fusion.140
  263.8 2.3 collective-permute-start.16
  268.6 2.6 collective-permute-done.17
  272.7 3.3 collective-permute-start.18
  276.0 2.3 collective-permute-start.19
  309.4 2.7 multiply_subtract_fusion.1
  325.7 2.3 multiply_reduce_fusion.6
  338.0 83.4 %psum.45 = f32[]{:T(128)} all-reduce(f32[]{:T(128)S(6)} %add.1442), channel_id=1, replica_groups=mesh['row'=16,'col'=16] {'row','col'}, use_global_device_ids=true, to_apply=%region_42.43 | all-reduce | flops 1 | bytes 8 | tf_op jit(solution)/shard_map/psum | solution.py:116
  425.9 2.2 collective-permute-start.20
  443.2 3.1 collective-permute-start.22
  449.4 2.1 collective-permute-done.23
  475.7 2.5 fusion.142
  479.0 4.9 collective-permute-start.24
  495.3 2.2 collective-permute-start.26
  497.5 2.9 collective-permute-start.27
  500.4 4.4 fusion.41
  538.0 2.5 multiply_subtract_fusion
  551.3 2.2 multiply_reduce_fusion
  578.4 81.8 %all-reduce = (f32[]{:T(128)}, f32[]{:T(128)}, f32[]{:T(128)}, f32[]{:T(128)}) all-reduce(f32[]{:T(128)S(6)} %sub.1093, f32[]{:T(128)S(6)} %sub.1044, f32[]{:T(128)S(6)} %sub.986, f32[]{:T(128)S(6)} %add.1554), channel_id=1, replica_groups=mesh['row'=16,'col'=16] {'row','col'}, use_global_device_ids=true, to_apply=%region_56.57 | all-reduce | flops 4 | bytes 32 | tf_op jit(solution)/shard_map/psum | solution.py:116
  (781 shorter events, 278.9 us)
Async XLA Ops:
  1.3 51.9 %collective-permute-start = (f32[3,1,32,64]{3,2,1,0:T(8,128)}, f32[3,1,32,64]{3,2,1,0:T(8,128)}, u32[]{:S(2)}, u32[]{:S(2)}) collective-permute-start(f32[3,1,32,64]{3,2,1,0:T(8,128)} %broadcast.870), channel_id=1, source_target_pairs={{0,16},{16,32},{32,48},{48,64},{64,80},{80,96},{96,112},{112,128},... | collective-permute-start | bytes 73736 | tf_op jit(solution)/shard_map/ppermute | solution.py:21
  6.2 47.0 %collective-permute-start.1 = (f32[3,1,32,64]{3,2,1,0:T(8,128)}, f32[3,1,32,64]{3,2,1,0:T(8,128)}, u32[]{:S(2)}, u32[]{:S(2)}) collective-permute-start(f32[3,1,32,64]{3,2,1,0:T(8,128)} %broadcast.870), channel_id=1, source_target_pairs={{16,0},{32,16},{48,32},{64,48},{80,64},{96,80},{112,96},{128,112},... | collective-permute-start | bytes 73736 | tf_op jit(solution)/shard_map/ppermute | solution.py:23
  8.5 30.2 %collective-permute-start.4 = (f32[1,32,64]{2,1,0:T(8,128)S(1)}, f32[1,32,64]{2,1,0:T(8,128)S(1)}, u32[]{:S(2)}, u32[]{:S(2)}) collective-permute-start(f32[1,32,64]{2,1,0:T(8,128)S(1)} %slice.1193), channel_id=1, source_target_pairs={{0,16},{16,32},{32,48},{48,64},{64,80},{80,96},{96,112},{112,128},... | collective-permute-start | bytes 24584 | tf_op jit(solution)/shard_map/ppermute | solution.py:21
  13.2 25.5 %collective-permute-start.5 = (f32[1,32,64]{2,1,0:T(8,128)}, f32[1,32,64]{2,1,0:T(8,128)S(1)}, u32[]{:S(2)}, u32[]{:S(2)}) collective-permute-start(f32[1,32,64]{2,1,0:T(8,128)} %slice.1195), channel_id=1, source_target_pairs={{16,0},{32,16},{48,32},{64,48},{80,64},{96,80},{112,96},{128,112},... | collective-permute-start | bytes 24584 | tf_op jit(solution)/shard_map/ppermute | solution.py:23
  18.8 204.2 %copy-start.180 = (f32[64]{0:T(128)}, f32[64]{0:T(128)S(1)}, u32[]{:S(2)}) copy-start(f32[64]{0:T(128)S(1)} %get-tuple-element.365) | copy-start | bytes 772
  18.8 205.3 %copy-start.178 = (f32[64]{0:T(128)}, f32[64]{0:T(128)S(1)}, u32[]{:S(2)}) copy-start(f32[64]{0:T(128)S(1)} %get-tuple-element.367) | copy-start | bytes 772
  18.8 205.3 %copy-start.182 = (f32[64]{0:T(128)}, f32[64]{0:T(128)S(1)}, u32[]{:S(2)}) copy-start(f32[64]{0:T(128)S(1)} %get-tuple-element.368) | copy-start | bytes 772
  28.0 196.2 %copy-start.29 = (f32[1,16,32,64]{3,2,1,0:T(8,128)}, f32[1,16,32,64]{3,2,1,0:T(8,128)S(1)}, u32[]{:S(2)}) copy-start(f32[1,16,32,64]{3,2,1,0:T(8,128)S(1)} %squeeze.619) | copy-start | bytes 393220
  40.0 8.0 %collective-permute-start.6 = (f32[18,1,64]{2,1,0:T(1,128)S(1)}, f32[18,1,64]{2,1,0:T(1,128)S(1)}, u32[]{:S(2)}, u32[]{:S(2)}) collective-permute-start(f32[18,1,64]{2,1,0:T(1,128)S(1)} %get-tuple-element.347), channel_id=1, source_target_pairs={{0,1},{1,2},{2,3},{3,4},{4,5},{5,6},{6,7},{7,8},{8,9},{9,10},{10,1... | collective-permute-start | bytes 13832 | tf_op jit(solution)/shard_map/ppermute | solution.py:21
  44.5 5.0 collective-permute-start.7
  54.1 6.0 collective-permute-start.2
  56.2 5.8 collective-permute-start.3
  86.0 9.5 %collective-permute-start.8 = (f32[3,1,32,64]{3,2,1,0:T(8,128)}, f32[3,1,32,64]{3,2,1,0:T(8,128)S(1)}, u32[]{:S(2)}, u32[]{:S(2)}) collective-permute-start(f32[3,1,32,64]{3,2,1,0:T(8,128)} %get-tuple-element.160), channel_id=1, source_target_pairs={{0,16},{16,32},{32,48},{48,64},{64,80},{80,96},{96,112},{112,128},... | collective-permute-start | bytes 73736 | tf_op jit(solution)/shard_map/ppermute | solution.py:21
  90.3 5.7 collective-permute-start.9
  96.6 9.3 %collective-permute-start.10 = (f32[3,18,1,64]{3,2,1,0:T(1,128)}, f32[3,18,1,64]{3,2,1,0:T(1,128)S(1)}, u32[]{:S(2)}, u32[]{:S(2)}) collective-permute-start(f32[3,18,1,64]{3,2,1,0:T(1,128)} %get-tuple-element.121), channel_id=1, source_target_pairs={{0,1},{1,2},{2,3},{3,4},{4,5},{5,6},{6,7},{7,8},{8,9},{9,10},{10,1... | collective-permute-start | bytes 41480 | tf_op jit(solution)/shard_map/ppermute | solution.py:21
  99.8 6.1 collective-permute-start.11
  224.9 5.0 collective-permute-start.12
  227.0 4.8 collective-permute-start.13
  231.9 5.9 collective-permute-start.14
  235.4 5.2 collective-permute-start.15
  263.8 4.8 collective-permute-start.16
  266.1 5.2 collective-permute-start.17
  272.7 22.6 %collective-permute-start.18 = (f32[3,18,1,64]{3,2,1,0:T(1,128)}, f32[3,18,1,64]{3,2,1,0:T(1,128)}, u32[]{:S(2)}, u32[]{:S(2)}) collective-permute-start(f32[3,18,1,64]{3,2,1,0:T(1,128)} %get-tuple-element.117), channel_id=1, source_target_pairs={{0,1},{1,2},{2,3},{3,4},{4,5},{5,6},{6,7},{7,8},{8,9},{9,10},{10,1... | collective-permute-start | bytes 41480 | tf_op jit(solution)/shard_map/ppermute | solution.py:21
  276.0 19.3 %collective-permute-start.19 = (f32[3,18,1,64]{3,2,1,0:T(1,128)}, f32[3,18,1,64]{3,2,1,0:T(1,128)}, u32[]{:S(2)}, u32[]{:S(2)}) collective-permute-start(f32[3,18,1,64]{3,2,1,0:T(1,128)} %get-tuple-element.118), channel_id=1, source_target_pairs={{1,0},{2,1},{3,2},{4,3},{5,4},{6,5},{7,6},{8,7},{9,8},{10,9},{11,1... | collective-permute-start | bytes 41480 | tf_op jit(solution)/shard_map/ppermute | solution.py:23
  425.9 16.4 %collective-permute-start.20 = (f32[3,1,32,64]{3,2,1,0:T(8,128)}, f32[3,1,32,64]{3,2,1,0:T(8,128)}, u32[]{:S(2)}, u32[]{:S(2)}) collective-permute-start(f32[3,1,32,64]{3,2,1,0:T(8,128)} %get-tuple-element.150), channel_id=1, source_target_pairs={{0,16},{16,32},{32,48},{48,64},{64,80},{80,96},{96,112},{112,128},... | collective-permute-start | bytes 73736 | tf_op jit(solution)/shard_map/ppermute | solution.py:21
  428.1 14.2 %collective-permute-start.21 = (f32[3,1,32,64]{3,2,1,0:T(8,128)}, f32[3,1,32,64]{3,2,1,0:T(8,128)}, u32[]{:S(2)}, u32[]{:S(2)}) collective-permute-start(f32[3,1,32,64]{3,2,1,0:T(8,128)} %get-tuple-element.151), channel_id=1, source_target_pairs={{16,0},{32,16},{48,32},{64,48},{80,64},{96,80},{112,96},{128,112},... | collective-permute-start | bytes 73736 | tf_op jit(solution)/shard_map/ppermute | solution.py:23
  443.2 6.2 collective-permute-start.22
  446.3 5.2 collective-permute-start.23
  479.0 14.4 %collective-permute-start.24 = (f32[3,1,32,64]{3,2,1,0:T(8,128)}, f32[3,1,32,64]{3,2,1,0:T(8,128)}, u32[]{:S(2)}, u32[]{:S(2)}) collective-permute-start(f32[3,1,32,64]{3,2,1,0:T(8,128)} %get-tuple-element.143), channel_id=1, source_target_pairs={{0,16},{16,32},{32,48},{48,64},{64,80},{80,96},{96,112},{112,128},... | collective-permute-start | bytes 73736 | tf_op jit(solution)/shard_map/ppermute | solution.py:21
  483.9 9.5 %collective-permute-start.25 = (f32[3,1,32,64]{3,2,1,0:T(8,128)}, f32[3,1,32,64]{3,2,1,0:T(8,128)}, u32[]{:S(2)}, u32[]{:S(2)}) collective-permute-start(f32[3,1,32,64]{3,2,1,0:T(8,128)} %get-tuple-element.144), channel_id=1, source_target_pairs={{16,0},{32,16},{48,32},{64,48},{80,64},{96,80},{112,96},{128,112},... | collective-permute-start | bytes 73736 | tf_op jit(solution)/shard_map/ppermute | solution.py:23
  495.3 27.7 %collective-permute-start.26 = (f32[3,18,1,64]{3,2,1,0:T(1,128)}, f32[3,18,1,64]{3,2,1,0:T(1,128)}, u32[]{:S(2)}, u32[]{:S(2)}) collective-permute-start(f32[3,18,1,64]{3,2,1,0:T(1,128)} %get-tuple-element.113), channel_id=1, source_target_pairs={{0,1},{1,2},{2,3},{3,4},{4,5},{5,6},{6,7},{7,8},{8,9},{9,10},{10,1... | collective-permute-start | bytes 41480 | tf_op jit(solution)/shard_map/ppermute | solution.py:21
  497.5 25.5 %collective-permute-start.27 = (f32[3,18,1,64]{3,2,1,0:T(1,128)}, f32[3,18,1,64]{3,2,1,0:T(1,128)}, u32[]{:S(2)}, u32[]{:S(2)}) collective-permute-start(f32[3,18,1,64]{3,2,1,0:T(1,128)} %get-tuple-element.114), channel_id=1, source_target_pairs={{1,0},{2,1},{3,2},{4,3},{5,4},{6,5},{7,6},{8,7},{9,8},{10,9},{11,1... | collective-permute-start | bytes 41480 | tf_op jit(solution)/shard_map/ppermute | solution.py:23
  (186 other events, 2931.7 us)
where the time goes:
time: 675 us; the launch traced here: 667 us
  blocking collectives  254 us (38%)
  local copies, waits for them, and re-layouts  125 us (19%)
  matrix products  87.9 us (13%)
  starting transfers between devices  72.2 us (11%)
  other arithmetic  66.3 us (10%)
  between operations  47.9 us (7%)
  waiting for transfers between devices  13.4 us (2%)
    psum x3, blocking collectives, shards(): total_squares, total_value = lax.psum((squares, value), ('row', 'col'))  254 us
    dot_general x171, matrix products, conv_valid(): jnp.dot(window, kernel[offset_row, offset_col], precision=lax.Precision.H...  87.9 us
    ppermute x14, starting transfers between devices, extended(): lax.ppermute(tail, axis, [(i, (i + 1) % count) for i in range(ends)])  46.5 us
    ppermute x14, starting transfers between devices, extended(): lax.ppermute(head, axis, [((i + 1) % count, i) for i in range(ends)])  25.6 us
    neg x15, local copies, waits for them, and re-layouts, shards(): coef = -conv_valid(dual_rim[layer], flipped(kernels[layer]))  21.6 us
  transfers between devices with their start and end apart: 28, of which 7 were waited for; matrix products, arithmetic and copies ran while one was open for 15% of the time, Pallas kernels for 0%

commit v1 on v0

--- a/solution.py
+++ b/solution.py
@@ -2,12 +2,19 @@
 import jax.numpy as jnp
 from jax import lax
 from jax.sharding import PartitionSpec as P
+from jax.lax import psum
 
 CH = 64
 LAYERS = 4
 ITERS = 3
 TEMP = 0.5
 EPS = 1e-06
+
+
+def things_mix(array_in, bus_axis, net_axis):
+    s_next = psum(array_in, axis_name=bus_axis)
+    outcome_arr = psum(s_next, axis_name=net_axis)
+    return outcome_arr
 
 
 def extended(cells, sides, width):
@@ -113,7 +120,7 @@
             squares = squares + jnp.sum(slope_dual * slope_dual) + jnp.sum(slope_mult * slope_mult)
             slope_duals.append(slope_dual)
             slope_mults.append(slope_mult)
-        total_squares, total_value = lax.psum((squares, value), ("row", "col"))
+        total_squares, total_value = things_mix((squares, value), "col", "row")
         bounds.append(total_value / total_cells)
         scale = step_sizes[step] / jnp.sqrt(total_squares / (2 * depth * total_cells) + EPS)
         duals = duals + scale * jnp.stack(slope_duals)

time: 675 us -> 643 us (0.953)
  the two profiles are of different devices: /device:TPU:1 before, /device:TPU:4 now
where the time goes in v1:
time: 643 us; the launch traced here: 634 us
  blocking collectives  211 us (33%)
  local copies, waits for them, and re-layouts  122 us (19%)
  starting transfers between devices  95.4 us (15%)
  matrix products  87.1 us (14%)
  other arithmetic  63.8 us (10%)
  between operations  47.6 us (7%)
  waiting for transfers between devices  6.76 us (1%)
    psum x3, blocking collectives, things_mix(): outcome_arr = psum(s_next, axis_name=net_axis)  121 us
    psum x3, blocking collectives, things_mix(): s_next = psum(array_in, axis_name=bus_axis)  90.1 us
    dot_general x171, matrix products, conv_valid(): jnp.dot(window, kernel[offset_row, offset_col], precision=lax.Precision.H...  87.1 us
    ppermute x14, starting transfers between devices, extended(): lax.ppermute(head, axis, [((i + 1) % count, i) for i in range(ends)])  62.3 us
    ppermute x14, starting transfers between devices, extended(): lax.ppermute(tail, axis, [(i, (i + 1) % count) for i in range(ends)])  33.1 us
    neg x15, local copies, waits for them, and re-layouts, shards(): coef = -conv_valid(dual_rim[layer], flipped(kernels[layer]))  20.7 us
    sub x7, other arithmetic, shards(): slope_mult = points[j + 1] - positive  13 us
  transfers between devices with their start and end apart: 28, of which 7 were waited for; matrix products, arithmetic and copies ran while one was open for 15% of the time, Pallas kernels for 0%

profile of v1, /device:TPU:4, one launch (start us, length us, event | category | flops | bytes accessed | tf_op | source)
XLA Modules:
  0.0 634.3 jit_solution(4564089453791105754)
XLA Ops:
  1.3 3.8 collective-permute-start
  5.1 5.8 collective-permute-start.1
  14.5 7.7 %collective-permute-start.5 = (f32[1,32,64]{2,1,0:T(8,128)}, f32[1,32,64]{2,1,0:T(8,128)S(1)}, u32[]{:S(2)}, u32[]{:S(2)}) collective-permute-start(f32[1,32,64]{2,1,0:T(8,128)} %slice.1195), channel_id=1, source_target_pairs={{16,0},{32,16},{48,32},{64,48},{80,64},{96,80},{112,96},{128,112},... | collective-permute-start | bytes 24584 | tf_op jit(solution)/shard_map/ppermute | solution.py:30
  49.0 2.6 collective-permute-done.7
  56.1 4.3 collective-permute-start.2
  87.9 7.5 %collective-permute-start.9 = (f32[3,1,32,64]{3,2,1,0:T(8,128)}, f32[3,1,32,64]{3,2,1,0:T(8,128)S(1)}, u32[]{:S(2)}, u32[]{:S(2)}) collective-permute-start(f32[3,1,32,64]{3,2,1,0:T(8,128)} %get-tuple-element.165), channel_id=1, source_target_pairs={{16,0},{32,16},{48,32},{64,48},{80,64},{96,80},{112,96},{128,112},... | collective-permute-start | bytes 73736 | tf_op jit(solution)/shard_map/ppermute | solution.py:30
  99.4 3.6 collective-permute-start.10
  104.5 2.3 multiply_reduce_fusion.14
  127.6 2.7 subtract_subtract_fusion.11
  134.1 32.0 %psum.86 = f32[]{:T(128)} all-reduce(f32[]{:T(128)S(6)} %add.1349), channel_id=1, replica_groups=mesh['row'=16,'col'=16] {'col'}, use_global_device_ids=true, to_apply=%region_22.23 | all-reduce | flops 1 | bytes 8 | tf_op jit(solution)/shard_map/psum | solution.py:15
  167.1 41.4 %psum.87 = f32[]{:T(128)} all-reduce(f32[]{:T(128)} %psum.86), channel_id=1, replica_groups=mesh['row'=16,'col'=16] {'row'}, use_global_device_ids=true, to_apply=%region_23.24 | all-reduce | flops 1 | bytes 8 | tf_op jit(solution)/shard_map/psum | solution.py:16
  211.8 2.1 collective-permute-start.12
  213.9 7.5 %collective-permute-start.13 = (f32[3,1,32,64]{3,2,1,0:T(8,128)S(1)}, f32[3,1,32,64]{3,2,1,0:T(8,128)S(1)}, u32[]{:S(2)}, u32[]{:S(2)}) collective-permute-start(f32[3,1,32,64]{3,2,1,0:T(8,128)S(1)} %get-tuple-element.163), channel_id=1, source_target_pairs={{16,0},{32,16},{48,32},{64,48},{80,64},{96,80},{112,96},{128,112},... | collective-permute-start | bytes 73736 | tf_op jit(solution)/shard_map/ppermute | solution.py:30
  247.8 2.4 fusion.140
  250.2 2.1 collective-permute-start.16
  252.2 7.9 %collective-permute-start.17 = (f32[3,1,32,64]{3,2,1,0:T(8,128)S(1)}, f32[3,1,32,64]{3,2,1,0:T(8,128)S(1)}, u32[]{:S(2)}, u32[]{:S(2)}) collective-permute-start(f32[3,1,32,64]{3,2,1,0:T(8,128)S(1)} %get-tuple-element.161), channel_id=1, source_target_pairs={{16,0},{32,16},{48,32},{64,48},{80,64},{96,80},{112,96},{128,112},... | collective-permute-start | bytes 73736 | tf_op jit(solution)/shard_map/ppermute | solution.py:30
  263.0 2.7 collective-permute-start.18
  298.1 2.6 multiply_subtract_fusion.1
  314.3 2.3 multiply_reduce_fusion.6
  327.0 29.2 %psum.90 = f32[]{:T(128)} all-reduce(f32[]{:T(128)S(6)} %add.1454), channel_id=1, replica_groups=mesh['row'=16,'col'=16] {'col'}, use_global_device_ids=true, to_apply=%region_45.46 | all-reduce | flops 1 | bytes 8 | tf_op jit(solution)/shard_map/psum | solution.py:15
  356.9 42.1 %psum.91 = f32[]{:T(128)} all-reduce(f32[]{:T(128)} %psum.90), channel_id=1, replica_groups=mesh['row'=16,'col'=16] {'row'}, use_global_device_ids=true, to_apply=%region_46.47 | all-reduce | flops 1 | bytes 8 | tf_op jit(solution)/shard_map/psum | solution.py:16
  406.4 7.7 %collective-permute-start.21 = (f32[3,1,32,64]{3,2,1,0:T(8,128)}, f32[3,1,32,64]{3,2,1,0:T(8,128)}, u32[]{:S(2)}, u32[]{:S(2)}) collective-permute-start(f32[3,1,32,64]{3,2,1,0:T(8,128)} %get-tuple-element.155), channel_id=1, source_target_pairs={{16,0},{32,16},{48,32},{64,48},{80,64},{96,80},{112,96},{128,112},... | collective-permute-start | bytes 73736 | tf_op jit(solution)/shard_map/ppermute | solution.py:30
  437.7 2.0 fusion.77
  456.4 2.5 fusion.142
  461.6 7.7 %collective-permute-start.25 = (f32[3,1,32,64]{3,2,1,0:T(8,128)}, f32[3,1,32,64]{3,2,1,0:T(8,128)}, u32[]{:S(2)}, u32[]{:S(2)}) collective-permute-start(f32[3,1,32,64]{3,2,1,0:T(8,128)} %get-tuple-element.148), channel_id=1, source_target_pairs={{16,0},{32,16},{48,32},{64,48},{80,64},{96,80},{112,96},{128,112},... | collective-permute-start | bytes 73736 | tf_op jit(solution)/shard_map/ppermute | solution.py:30
  469.3 2.1 fusion.69
  479.2 3.0 collective-permute-start.26
  483.7 4.4 fusion.41
  521.2 2.5 multiply_subtract_fusion
  534.5 2.2 multiply_reduce_fusion
  561.4 28.9 %all-reduce = (f32[]{:T(128)}, f32[]{:T(128)}, f32[]{:T(128)}, f32[]{:T(128)}) all-reduce(f32[]{:T(128)S(6)} %sub.1093, f32[]{:T(128)S(6)} %sub.1044, f32[]{:T(128)S(6)} %sub.986, f32[]{:T(128)S(6)} %add.1566), channel_id=1, replica_groups=mesh['row'=16,'col'=16] {'col'}, use_global_device_ids=true, to_apply=%region_60.61 | all-reduce | flops 4 | bytes 32 | tf_op jit(solution)/shard_map/psum | solution.py:15
  590.4 37.6 %all-reduce.1 = (f32[]{:T(128)}, f32[]{:T(128)}, f32[]{:T(128)}, f32[]{:T(128)}) all-reduce(f32[]{:T(128)} %get-tuple-element.56, f32[]{:T(128)} %get-tuple-element.57, f32[]{:T(128)} %get-tuple-element.58, f32[]{:T(128)} %get-tuple-element.59), channel_id=1, replica_groups=mesh['row'=16,'col'=16] {'row'}, use_global_device_ids=true, to_apply=%region_61.62 | all-reduce | flops 4 | bytes 32 | tf_op jit(solution)/shard_map/psum | solution.py:16
  (800 shorter events, 271.7 us)
Async XLA Ops:
  1.3 54.0 %collective-permute-start = (f32[3,1,32,64]{3,2,1,0:T(8,128)}, f32[3,1,32,64]{3,2,1,0:T(8,128)}, u32[]{:S(2)}, u32[]{:S(2)}) collective-permute-start(f32[3,1,32,64]{3,2,1,0:T(8,128)} %broadcast.870), channel_id=1, source_target_pairs={{0,16},{16,32},{32,48},{48,64},{64,80},{80,96},{96,112},{112,128},... | collective-permute-start | bytes 73736 | tf_op jit(solution)/shard_map/ppermute | solution.py:28
  5.1 50.2 %collective-permute-start.1 = (f32[3,1,32,64]{3,2,1,0:T(8,128)}, f32[3,1,32,64]{3,2,1,0:T(8,128)}, u32[]{:S(2)}, u32[]{:S(2)}) collective-permute-start(f32[3,1,32,64]{3,2,1,0:T(8,128)} %broadcast.870), channel_id=1, source_target_pairs={{16,0},{32,16},{48,32},{64,48},{80,64},{96,80},{112,96},{128,112},... | collective-permute-start | bytes 73736 | tf_op jit(solution)/shard_map/ppermute | solution.py:30
  11.9 31.6 %collective-permute-start.4 = (f32[1,32,64]{2,1,0:T(8,128)S(1)}, f32[1,32,64]{2,1,0:T(8,128)S(1)}, u32[]{:S(2)}, u32[]{:S(2)}) collective-permute-start(f32[1,32,64]{2,1,0:T(8,128)S(1)} %slice.1193), channel_id=1, source_target_pairs={{0,16},{16,32},{32,48},{48,64},{64,80},{80,96},{96,112},{112,128},... | collective-permute-start | bytes 24584 | tf_op jit(solution)/shard_map/ppermute | solution.py:28
  14.5 29.1 %collective-permute-start.5 = (f32[1,32,64]{2,1,0:T(8,128)}, f32[1,32,64]{2,1,0:T(8,128)S(1)}, u32[]{:S(2)}, u32[]{:S(2)}) collective-permute-start(f32[1,32,64]{2,1,0:T(8,128)} %slice.1195), channel_id=1, source_target_pairs={{16,0},{32,16},{48,32},{64,48},{80,64},{96,80},{112,96},{128,112},... | collective-permute-start | bytes 24584 | tf_op jit(solution)/shard_map/ppermute | solution.py:30
  26.3 183.5 %copy-start.188 = (f32[64]{0:T(128)}, f32[64]{0:T(128)S(1)}, u32[]{:S(2)}) copy-start(f32[64]{0:T(128)S(1)} %get-tuple-element.369) | copy-start | bytes 772
  26.3 184.7 %copy-start.186 = (f32[64]{0:T(128)}, f32[64]{0:T(128)S(1)}, u32[]{:S(2)}) copy-start(f32[64]{0:T(128)S(1)} %get-tuple-element.371) | copy-start | bytes 772
  26.3 184.7 %copy-start.190 = (f32[64]{0:T(128)}, f32[64]{0:T(128)S(1)}, u32[]{:S(2)}) copy-start(f32[64]{0:T(128)S(1)} %get-tuple-element.372) | copy-start | bytes 772
  35.6 175.5 %copy-start.29 = (f32[1,16,32,64]{3,2,1,0:T(8,128)}, f32[1,16,32,64]{3,2,1,0:T(8,128)S(1)}, u32[]{:S(2)}) copy-start(f32[1,16,32,64]{3,2,1,0:T(8,128)S(1)} %squeeze.619) | copy-start | bytes 393220
  44.8 4.1 collective-permute-start.6
  46.1 5.4 collective-permute-start.7
  56.1 7.2 %collective-permute-start.2 = (f32[3,18,1,64]{3,2,1,0:T(1,128)S(1)}, f32[3,18,1,64]{3,2,1,0:T(1,128)S(1)}, u32[]{:S(2)}, u32[]{:S(2)}) collective-permute-start(f32[3,18,1,64]{3,2,1,0:T(1,128)S(1)} %get-tuple-element.127), channel_id=1, source_target_pairs={{0,1},{1,2},{2,3},{3,4},{4,5},{5,6},{6,7},{7,8},{8,9},{9,10},{10,1... | collective-permute-start | bytes 41480 | tf_op jit(solution)/shard_map/ppermute | solution.py:28
  60.5 3.1 collective-permute-start.3
  86.0 12.7 %collective-permute-start.8 = (f32[3,1,32,64]{3,2,1,0:T(8,128)}, f32[3,1,32,64]{3,2,1,0:T(8,128)S(1)}, u32[]{:S(2)}, u32[]{:S(2)}) collective-permute-start(f32[3,1,32,64]{3,2,1,0:T(8,128)} %get-tuple-element.164), channel_id=1, source_target_pairs={{0,16},{16,32},{32,48},{48,64},{64,80},{80,96},{96,112},{112,128},... | collective-permute-start | bytes 73736 | tf_op jit(solution)/shard_map/ppermute | solution.py:28
  87.9 10.8 %collective-permute-start.9 = (f32[3,1,32,64]{3,2,1,0:T(8,128)}, f32[3,1,32,64]{3,2,1,0:T(8,128)S(1)}, u32[]{:S(2)}, u32[]{:S(2)}) collective-permute-start(f32[3,1,32,64]{3,2,1,0:T(8,128)} %get-tuple-element.165), channel_id=1, source_target_pairs={{16,0},{32,16},{48,32},{64,48},{80,64},{96,80},{112,96},{128,112},... | collective-permute-start | bytes 73736 | tf_op jit(solution)/shard_map/ppermute | solution.py:30
  99.4 9.1 %collective-permute-start.10 = (f32[3,18,1,64]{3,2,1,0:T(1,128)}, f32[3,18,1,64]{3,2,1,0:T(1,128)S(1)}, u32[]{:S(2)}, u32[]{:S(2)}) collective-permute-start(f32[3,18,1,64]{3,2,1,0:T(1,128)} %get-tuple-element.125), channel_id=1, source_target_pairs={{0,1},{1,2},{2,3},{3,4},{4,5},{5,6},{6,7},{7,8},{8,9},{9,10},{10,1... | collective-permute-start | bytes 41480 | tf_op jit(solution)/shard_map/ppermute | solution.py:28
  103.0 5.5 collective-permute-start.11
  211.8 9.7 %collective-permute-start.12 = (f32[3,1,32,64]{3,2,1,0:T(8,128)S(1)}, f32[3,1,32,64]{3,2,1,0:T(8,128)S(1)}, u32[]{:S(2)}, u32[]{:S(2)}) collective-permute-start(f32[3,1,32,64]{3,2,1,0:T(8,128)S(1)} %get-tuple-element.162), channel_id=1, source_target_pairs={{0,16},{16,32},{32,48},{48,64},{64,80},{80,96},{96,112},{112,128},... | collective-permute-start | bytes 73736 | tf_op jit(solution)/shard_map/ppermute | solution.py:28
  213.9 9.3 %collective-permute-start.13 = (f32[3,1,32,64]{3,2,1,0:T(8,128)S(1)}, f32[3,1,32,64]{3,2,1,0:T(8,128)S(1)}, u32[]{:S(2)}, u32[]{:S(2)}) collective-permute-start(f32[3,1,32,64]{3,2,1,0:T(8,128)S(1)} %get-tuple-element.163), channel_id=1, source_target_pairs={{16,0},{32,16},{48,32},{64,48},{80,64},{96,80},{112,96},{128,112},... | collective-permute-start | bytes 73736 | tf_op jit(solution)/shard_map/ppermute | solution.py:30
  223.2 2.9 collective-permute-start.14
  224.5 3.1 collective-permute-start.15
  250.2 11.6 %collective-permute-start.16 = (f32[3,1,32,64]{3,2,1,0:T(8,128)S(1)}, f32[3,1,32,64]{3,2,1,0:T(8,128)S(1)}, u32[]{:S(2)}, u32[]{:S(2)}) collective-permute-start(f32[3,1,32,64]{3,2,1,0:T(8,128)S(1)} %get-tuple-element.160), channel_id=1, source_target_pairs={{0,16},{16,32},{32,48},{48,64},{64,80},{80,96},{96,112},{112,128},... | collective-permute-start | bytes 73736 | tf_op jit(solution)/shard_map/ppermute | solution.py:28
  252.2 9.6 %collective-permute-start.17 = (f32[3,1,32,64]{3,2,1,0:T(8,128)S(1)}, f32[3,1,32,64]{3,2,1,0:T(8,128)S(1)}, u32[]{:S(2)}, u32[]{:S(2)}) collective-permute-start(f32[3,1,32,64]{3,2,1,0:T(8,128)S(1)} %get-tuple-element.161), channel_id=1, source_target_pairs={{16,0},{32,16},{48,32},{64,48},{80,64},{96,80},{112,96},{128,112},... | collective-permute-start | bytes 73736 | tf_op jit(solution)/shard_map/ppermute | solution.py:30
  263.0 21.0 %collective-permute-start.18 = (f32[3,18,1,64]{3,2,1,0:T(1,128)}, f32[3,18,1,64]{3,2,1,0:T(1,128)}, u32[]{:S(2)}, u32[]{:S(2)}) collective-permute-start(f32[3,18,1,64]{3,2,1,0:T(1,128)} %get-tuple-element.121), channel_id=1, source_target_pairs={{0,1},{1,2},{2,3},{3,4},{4,5},{5,6},{6,7},{7,8},{8,9},{9,10},{10,1... | collective-permute-start | bytes 41480 | tf_op jit(solution)/shard_map/ppermute | solution.py:28
  265.7 18.4 %collective-permute-start.19 = (f32[3,18,1,64]{3,2,1,0:T(1,128)}, f32[3,18,1,64]{3,2,1,0:T(1,128)}, u32[]{:S(2)}, u32[]{:S(2)}) collective-permute-start(f32[3,18,1,64]{3,2,1,0:T(1,128)} %get-tuple-element.122), channel_id=1, source_target_pairs={{1,0},{2,1},{3,2},{4,3},{5,4},{6,5},{7,6},{8,7},{9,8},{10,9},{11,1... | collective-permute-start | bytes 41480 | tf_op jit(solution)/shard_map/ppermute | solution.py:30
  404.5 22.4 %collective-permute-start.20 = (f32[3,1,32,64]{3,2,1,0:T(8,128)}, f32[3,1,32,64]{3,2,1,0:T(8,128)}, u32[]{:S(2)}, u32[]{:S(2)}) collective-permute-start(f32[3,1,32,64]{3,2,1,0:T(8,128)} %get-tuple-element.154), channel_id=1, source_target_pairs={{0,16},{16,32},{32,48},{48,64},{64,80},{80,96},{96,112},{112,128},... | collective-permute-start | bytes 73736 | tf_op jit(solution)/shard_map/ppermute | solution.py:28
  406.4 20.4 %collective-permute-start.21 = (f32[3,1,32,64]{3,2,1,0:T(8,128)}, f32[3,1,32,64]{3,2,1,0:T(8,128)}, u32[]{:S(2)}, u32[]{:S(2)}) collective-permute-start(f32[3,1,32,64]{3,2,1,0:T(8,128)} %get-tuple-element.155), channel_id=1, source_target_pairs={{16,0},{32,16},{48,32},{64,48},{80,64},{96,80},{112,96},{128,112},... | collective-permute-start | bytes 73736 | tf_op jit(solution)/shard_map/ppermute | solution.py:30
  427.7 3.7 collective-permute-start.22
  429.0 3.1 collective-permute-start.23
  459.7 17.7 %collective-permute-start.24 = (f32[3,1,32,64]{3,2,1,0:T(8,128)}, f32[3,1,32,64]{3,2,1,0:T(8,128)}, u32[]{:S(2)}, u32[]{:S(2)}) collective-permute-start(f32[3,1,32,64]{3,2,1,0:T(8,128)} %get-tuple-element.147), channel_id=1, source_target_pairs={{0,16},{16,32},{32,48},{48,64},{64,80},{80,96},{96,112},{112,128},... | collective-permute-start | bytes 73736 | tf_op jit(solution)/shard_map/ppermute | solution.py:28
  461.6 15.8 %collective-permute-start.25 = (f32[3,1,32,64]{3,2,1,0:T(8,128)}, f32[3,1,32,64]{3,2,1,0:T(8,128)}, u32[]{:S(2)}, u32[]{:S(2)}) collective-permute-start(f32[3,1,32,64]{3,2,1,0:T(8,128)} %get-tuple-element.148), channel_id=1, source_target_pairs={{16,0},{32,16},{48,32},{64,48},{80,64},{96,80},{112,96},{128,112},... | collective-permute-start | bytes 73736 | tf_op jit(solution)/shard_map/ppermute | solution.py:30
  479.2 26.9 %collective-permute-start.26 = (f32[3,18,1,64]{3,2,1,0:T(1,128)}, f32[3,18,1,64]{3,2,1,0:T(1,128)}, u32[]{:S(2)}, u32[]{:S(2)}) collective-permute-start(f32[3,18,1,64]{3,2,1,0:T(1,128)} %get-tuple-element.117), channel_id=1, source_target_pairs={{0,1},{1,2},{2,3},{3,4},{4,5},{5,6},{6,7},{7,8},{8,9},{9,10},{10,1... | collective-permute-start | bytes 41480 | tf_op jit(solution)/shard_map/ppermute | solution.py:28
  482.2 23.9 %collective-permute-start.27 = (f32[3,18,1,64]{3,2,1,0:T(1,128)}, f32[3,18,1,64]{3,2,1,0:T(1,128)}, u32[]{:S(2)}, u32[]{:S(2)}) collective-permute-start(f32[3,18,1,64]{3,2,1,0:T(1,128)} %get-tuple-element.118), channel_id=1, source_target_pairs={{1,0},{2,1},{3,2},{4,3},{5,4},{6,5},{7,6},{8,7},{9,8},{10,9},{11,1... | collective-permute-start | bytes 41480 | tf_op jit(solution)/shard_map/ppermute | solution.py:30
  (194 other events, 2799.2 us)
